TPU v7x, 32 devices: a whole 2x2x4 slice. The times are simulated.
32 devices in a mesh: shard: 4 (over y, core), context: 2 (over x), tensor: 4 (over z).
Axes of the slice: x: 2, y: 2, z: 4, core: 2. Of those that a mesh axis runs over, the one named last changes fastest.
Arguments:
- block_input: bfloat16 [8192, 1536], P(('shard', 'context')), may hold values from -6 to 6
- norm_gain: float32 [1536], replicated, may hold values from 0.5 to 1.5
- w_z: bfloat16 [1536, 3072], P('shard', 'tensor'), may hold values from -0.15625 to 0.15625
- w_x: bfloat16 [1536, 3072], P('shard', 'tensor'), may hold values from -0.15625 to 0.15625
- w_bc: bfloat16 [1536, 256], P('shard'), may hold values from -0.15625 to 0.15625
- w_dt: bfloat16 [1536, 48], P('shard', 'tensor'), may hold values from -0.15625 to 0.15625
- conv_x_weight: float32 [4, 3072], P(None, 'tensor'), may hold values from -3 to 3
- conv_x_bias: float32 [3072], P('tensor'), may hold values from -1.5 to 1.5
- conv_bc_weight: float32 [4, 256], replicated, may hold values from -3 to 3
- conv_bc_bias: float32 [256], replicated, may hold values from -1.5 to 1.5
- dt_bias: float32 [48], P('tensor'), may hold values from -4 to -1
- a_log: float32 [48], P('tensor'), may hold values from -9 to 0
- d_skip: float32 [48], P('tensor'), may hold values from 0.5 to 1.5
- gate_gain: float32 [3072], P('tensor'), may hold values from 0.5 to 1.5
- w_out: bfloat16 [3072, 1536], P('tensor', 'shard'), may hold values from -0.109375 to 0.109375
- out_cotangent: bfloat16 [8192, 1536], P(('shard', 'context')), may hold values from -6 to 6
Outputs:
- block_output: bfloat16 [8192, 1536], P(('shard', 'context'))
- input_grad: float32 [8192, 1536], P(('shard', 'context'))
- grad_w_z: float32 [1536, 3072], P(('shard', 'context'), 'tensor')
- grad_w_x: float32 [1536, 3072], P(('shard', 'context'), 'tensor')
- grad_w_bc: float32 [1536, 256], P(('shard', 'context'))
- grad_w_dt: float32 [1536, 48], P(('shard', 'context'), 'tensor')
- grad_w_out: float32 [3072, 1536], P('tensor', ('shard', 'context'))
- grad_norm_gain: float32 [1536], replicated
- grad_conv_x_weight: float32 [4, 3072], P(None, 'tensor')
- grad_conv_x_bias: float32 [3072], P('tensor')
- grad_conv_bc_weight: float32 [4, 256], replicated
- grad_conv_bc_bias: float32 [256], replicated
- grad_dt_bias: float32 [48], P('tensor')
- grad_a_log: float32 [48], P('tensor')
- grad_d_skip: float32 [48], P('tensor')
- grad_gate_gain: float32 [3072], P('tensor')
All inputs are finite; a program needn't handle non-finite values.
Results may differ from a plain program's by a relative error of at most 0.0021.
The roundings to bfloat16 on the way count: a program that leaves them out, or rounds other values in their place, can miss the bound.
Values may be sent and summed in bfloat16 or wider, within the bound.
No kernel may reach another device: no remote copies, remote signals or barrier semaphores. Data moves between devices by JAX's collectives and lax.ppermute only.
A program may use at most 192 MiB of HBM per device.

v0:
```python
import jax
import jax.numpy as jnp
from jax import lax
from jax.sharding import PartitionSpec as P

HEADS = 48
HEAD_DIM = 64
STATE = 128
CONV = 4
GROUP = 256
epsilon = 1e-05
precise = lax.Precision.HIGHEST


def shifted(shard, axis, by):
    length = lax.axis_size(axis)
    pairs = [(i, i + by) for i in range(length) if 0 <= i + by < length]
    return lax.ppermute(shard, axis, pairs)


def prefix(value, axis, join, neutral, backward):
    count, mine = (lax.axis_size(axis), lax.axis_index(axis))
    pieces = jax.tree.map(lambda part: lax.all_gather(part, axis), value)
    if backward:
        pieces = jax.tree.map(lambda part: part[::-1], pieces)
        mine = count - 1 - mine
    running = jax.tree.map(
        lambda part, zero: jnp.full_like(part, 0) + jnp.asarray(zero, part.dtype), value, neutral
    )

    def hop(position, running):
        longer = join(running, jax.tree.map(lambda part: part[position], pieces))
        return jax.tree.map(lambda new, old: jnp.where(position < mine, new, old), longer, running)

    return lax.fori_loop(0, count - 1, hop, running)


def silu_slope(value):
    sigma = jax.nn.sigmoid(value)
    return sigma * (1.0 + value * (1.0 - sigma))


def group_states(x_conv, step_size, decay_rate, b_mat, span):
    length, heads, width = x_conv.shape
    count = length // span
    log_step = (-step_size * decay_rate[None, :]).reshape(count, span, heads)
    cum_log = jnp.cumsum(log_step, axis=1)
    x_step = (x_conv * step_size[:, :, None]).reshape(count, span, heads, width)
    tail = jnp.exp(cum_log[:, -1:, :] - cum_log)
    states = jnp.einsum(
        "cqhp,cqn->chpn",
        x_step * tail[:, :, :, None],
        b_mat.reshape(count, span, -1),
        precision=precise,
    )
    return (cum_log, x_step, states)


def summarize(cum_log, states):
    totals = cum_log[:, -1, :]

    def advance(carry, item):
        total, state = item
        return (jnp.exp(total)[:, None, None] * carry + state, carry)

    final, enter = lax.scan(advance, jnp.zeros(states.shape[1:], jnp.float32), (totals, states))
    return (enter, jnp.sum(totals, axis=0), final)


def entry_scale(cum_log):
    totals = cum_log[:, -1, :]
    return jnp.exp(jnp.cumsum(totals, axis=0) - totals)


def group_output(cum_log, x_step, b_mat, c_mat, enter):
    count, span, heads, width = x_step.shape
    b_view = b_mat.reshape(count, span, -1)
    c_view = c_mat.reshape(count, span, -1)
    scores = jnp.einsum("ctn,csn->cts", c_view, b_view, precision=precise)
    cum_heads = jnp.transpose(cum_log, (0, 2, 1))
    gaps = cum_heads[:, :, :, None] - cum_heads[:, :, None, :]
    lower = jnp.arange(span)[:, None] >= jnp.arange(span)[None, :]
    decay = jnp.where(lower, jnp.exp(jnp.minimum(gaps, 0.0)), 0.0)
    inner = jnp.einsum("chts,cshp->cthp", decay * scores[:, None], x_step, precision=precise)
    outer = (
        jnp.einsum("ctn,chpn->cthp", c_view, enter, precision=precise)
        * jnp.exp(cum_log)[:, :, :, None]
    )
    return (inner + outer).reshape(count * span, heads, width)


def ssd_local(x_conv, step_size, decay_rate, b_mat, c_mat, s_in):
    span = min(GROUP, x_conv.shape[0])
    cum_log, x_step, states = group_states(x_conv, step_size, decay_rate, b_mat, span)
    enter, log_decay, s_local = summarize(cum_log, states)
    before = entry_scale(cum_log)
    enter = enter + before[:, :, None, None] * s_in[None]
    return (group_output(cum_log, x_step, b_mat, c_mat, enter), log_decay, s_local)


def combine_carry(earlier, later):
    return (earlier[0] + later[0], earlier[1] * jnp.exp(later[0])[:, None, None] + later[1])


def conv_apply(padded, conv_weight, conv_bias, length):
    total = conv_bias[None, :] + conv_weight[0] * padded[0:length]
    for offset in range(1, CONV):
        total = total + conv_weight[offset] * padded[offset : offset + length]
    return total


def conv_transpose(grad_pre, conv_weight):
    total = jnp.pad(conv_weight[0] * grad_pre, ((0, CONV - 1), (0, 0)))
    for offset in range(1, CONV):
        total = total + jnp.pad(
            conv_weight[offset] * grad_pre, ((offset, CONV - 1 - offset), (0, 0))
        )
    return total


def shards(
    block_input,
    norm_gain,
    w_z,
    w_x,
    w_bc,
    w_dt,
    conv_x_weight,
    conv_x_bias,
    conv_bc_weight,
    conv_bc_bias,
    dt_bias,
    a_log,
    d_skip,
    gate_gain,
    w_out,
    out_cotangent,
):
    full_z, full_x, full_bc, full_dt, full_out = (
        lax.all_gather(w_z, "shard", axis=0, tiled=True),
        lax.all_gather(w_x, "shard", axis=0, tiled=True),
        lax.all_gather(w_bc, "shard", axis=0, tiled=True),
        lax.all_gather(w_dt, "shard", axis=0, tiled=True),
        lax.all_gather(w_out, "shard", axis=1, tiled=True),
    )
    length = block_input.shape[0]
    local_inner = w_z.shape[1]
    heads_here = w_dt.shape[1]
    inner_width = HEADS * HEAD_DIM
    x_float = block_input.astype(jnp.float32)
    inverse = lax.rsqrt(jnp.mean(x_float * x_float, axis=1, keepdims=True) + epsilon)
    normed = (x_float * inverse * norm_gain).astype(jnp.bfloat16)
    z_part = jnp.dot(normed, full_z, preferred_element_type=jnp.float32)
    x_raw = jnp.dot(normed, full_x, preferred_element_type=jnp.float32).astype(jnp.bfloat16)
    bc_raw = jnp.dot(normed, full_bc, preferred_element_type=jnp.float32).astype(jnp.bfloat16)
    dt_raw = jnp.dot(normed, full_dt, preferred_element_type=jnp.float32)
    conv_in = jnp.concatenate([x_raw, bc_raw], axis=1)
    edge = shifted(conv_in[length - CONV + 1 :], "context", 1)
    padded = jnp.concatenate([edge, conv_in], axis=0).astype(jnp.float32)
    conv_weight = jnp.concatenate([conv_x_weight, conv_bc_weight], axis=1)
    conv_bias = jnp.concatenate([conv_x_bias, conv_bc_bias])
    pre = conv_apply(padded, conv_weight, conv_bias, length)
    act = jax.nn.silu(pre)
    x_conv = act[:, :local_inner].reshape(length, heads_here, HEAD_DIM)
    b_mat = act[:, local_inner : local_inner + STATE]
    c_mat = act[:, local_inner + STATE :]
    step_size = jax.nn.softplus(dt_raw + dt_bias)
    decay_rate = jnp.exp(a_log)
    span = min(GROUP, length)
    cum_log, x_step, states = group_states(x_conv, step_size, decay_rate, b_mat, span)
    enter, log_decay, s_local = summarize(cum_log, states)
    identity = (jnp.zeros_like(log_decay), jnp.zeros_like(s_local))
    s_in = prefix((log_decay, s_local), "context", combine_carry, identity, False)[1]
    before = entry_scale(cum_log)
    enter = enter + before[:, :, None, None] * s_in[None]
    ssd_out = group_output(cum_log, x_step, b_mat, c_mat, enter)
    mixer = (ssd_out + d_skip[None, :, None] * x_conv).reshape(length, local_inner)
    gate_value = jax.nn.silu(z_part)
    gated = mixer * gate_value
    square_sum = lax.psum(jnp.sum(gated * gated, axis=1), "tensor")
    gate_inverse = lax.rsqrt(square_sum[:, None] / inner_width + epsilon)
    gated_out = (gated * gate_inverse * gate_gain).astype(jnp.bfloat16)
    out_part = jnp.dot(gated_out, full_out, preferred_element_type=jnp.float32)
    out_total = lax.psum(out_part, "tensor")
    block_output = (x_float + out_total).astype(jnp.bfloat16)
    grad_gated_out = jnp.einsum(
        "td,kd->tk", out_cotangent, full_out, preferred_element_type=jnp.float32
    )
    grad_w_out = jnp.einsum(
        "tk,td->kd", gated_out, out_cotangent, preferred_element_type=jnp.float32
    )
    scaled = gate_gain * grad_gated_out
    row_terms = lax.psum(jnp.sum(scaled * gated, axis=1), "tensor")
    grad_gated = gate_inverse * scaled - gated * gate_inverse * gate_inverse * gate_inverse * (
        row_terms[:, None] / inner_width
    )
    grad_gate_gain = jnp.sum(grad_gated_out * gated * gate_inverse, axis=0)
    grad_mixer = grad_gated * gate_value
    grad_z = (grad_gated * mixer * silu_slope(z_part)).astype(jnp.bfloat16)
    grad_heads = grad_mixer.reshape(length, heads_here, HEAD_DIM)
    grad_d_skip = jnp.sum(grad_heads * x_conv, axis=(0, 2))
    count = length // span
    weighted = (
        grad_heads.reshape(count, span, heads_here, HEAD_DIM)
        * (jnp.exp(cum_log) * before[:, None, :])[:, :, :, None]
    )
    own_grad = jnp.einsum(
        "cqhp,cqn->hpn", weighted, c_mat.reshape(count, span, STATE), precision=precise
    )
    carried = prefix((log_decay, own_grad), "context", combine_carry, identity, True)[1]
    grad_decay = jnp.sum(carried * s_in, axis=(1, 2)) * jnp.exp(log_decay)
    unused_out, pullback = jax.vjp(ssd_local, x_conv, step_size, decay_rate, b_mat, c_mat, s_in)
    grad_xc, grad_step, grad_rate, grad_b, grad_c, unused_state = pullback(
        (grad_heads, grad_decay, carried)
    )
    grad_xc = grad_xc + d_skip[None, :, None] * grad_heads
    grad_bc = lax.psum(jnp.concatenate([grad_b, grad_c], axis=1), "tensor")
    grad_act = jnp.concatenate([grad_xc.reshape(length, local_inner), grad_bc], axis=1)
    grad_pre = grad_act * silu_slope(pre)
    grad_conv_bias = jnp.sum(grad_pre, axis=0)
    grad_conv_weight = jnp.stack(
        [jnp.sum(grad_pre * padded[offset : offset + length], axis=0) for offset in range(CONV)]
    )
    grad_padded = conv_transpose(grad_pre, conv_weight)
    back_edge = shifted(grad_padded[: CONV - 1], "context", -1)
    grad_conv_in = grad_padded[CONV - 1 :] + jnp.pad(back_edge, ((length - CONV + 1, 0), (0, 0)))
    grad_x_raw = grad_conv_in[:, :local_inner].astype(jnp.bfloat16)
    grad_bc_raw = grad_conv_in[:, local_inner:].astype(jnp.bfloat16)
    slope = jax.nn.sigmoid(dt_raw + dt_bias)
    grad_dt_bias = jnp.sum(grad_step * slope, axis=0)
    grad_dt_raw = (grad_step * slope).astype(jnp.bfloat16)
    grad_a_log = grad_rate * decay_rate
    partial_normed = (
        jnp.einsum("tk,dk->td", grad_z, full_z, preferred_element_type=jnp.float32)
        + jnp.einsum("tk,dk->td", grad_x_raw, full_x, preferred_element_type=jnp.float32)
        + jnp.einsum("tk,dk->td", grad_dt_raw, full_dt, preferred_element_type=jnp.float32)
    )
    grad_normed = lax.psum(partial_normed, "tensor") + jnp.einsum(
        "tk,dk->td", grad_bc_raw, full_bc, preferred_element_type=jnp.float32
    )
    scaled_in = norm_gain * grad_normed
    input_grad = (
        out_cotangent.astype(jnp.float32)
        + inverse * scaled_in
        - x_float
        * inverse
        * inverse
        * inverse
        * jnp.mean(scaled_in * x_float, axis=1, keepdims=True)
    )
    grad_norm_gain = jnp.sum(grad_normed * x_float * inverse, axis=0)
    grad_w_z = jnp.einsum("td,tk->dk", normed, grad_z, preferred_element_type=jnp.float32)
    grad_w_x = jnp.einsum("td,tk->dk", normed, grad_x_raw, preferred_element_type=jnp.float32)
    grad_w_bc = jnp.einsum("td,tk->dk", normed, grad_bc_raw, preferred_element_type=jnp.float32)
    grad_w_dt = jnp.einsum("td,tk->dk", normed, grad_dt_raw, preferred_element_type=jnp.float32)
    summed_z, summed_x, summed_bc, summed_dt, summed_out = (
        lax.psum_scatter(grad_w_z, ("shard", "context"), scatter_dimension=0, tiled=True),
        lax.psum_scatter(grad_w_x, ("shard", "context"), scatter_dimension=0, tiled=True),
        lax.psum_scatter(grad_w_bc, ("shard", "context"), scatter_dimension=0, tiled=True),
        lax.psum_scatter(grad_w_dt, ("shard", "context"), scatter_dimension=0, tiled=True),
        lax.psum_scatter(grad_w_out, ("shard", "context"), scatter_dimension=1, tiled=True),
    )
    (
        sum_norm_gain,
        sum_conv_x_weight,
        sum_conv_x_bias,
        sum_conv_bc_weight,
        sum_conv_bc_bias,
        sum_dt_bias,
        sum_a_log,
        sum_d_skip,
        sum_gate_gain,
    ) = lax.psum(
        (
            grad_norm_gain,
            grad_conv_weight[:, :local_inner],
            grad_conv_bias[:local_inner],
            grad_conv_weight[:, local_inner:],
            grad_conv_bias[local_inner:],
            grad_dt_bias,
            grad_a_log,
            grad_d_skip,
            grad_gate_gain,
        ),
        ("shard", "context"),
    )
    return (
        block_output,
        input_grad,
        summed_z,
        summed_x,
        summed_bc,
        summed_dt,
        summed_out,
        sum_norm_gain,
        sum_conv_x_weight,
        sum_conv_x_bias,
        sum_conv_bc_weight,
        sum_conv_bc_bias,
        sum_dt_bias,
        sum_a_log,
        sum_d_skip,
        sum_gate_gain,
    )


def solution(mesh):
    in_specs = (
        P(("shard", "context"), None),
        P(),
        P("shard", "tensor"),
        P("shard", "tensor"),
        P("shard", None),
        P("shard", "tensor"),
        P(None, "tensor"),
        P("tensor"),
        P(),
        P(),
        P("tensor"),
        P("tensor"),
        P("tensor"),
        P("tensor"),
        P("tensor", "shard"),
        P(("shard", "context"), None),
    )
    out_specs = (
        P(("shard", "context"), None),
        P(("shard", "context"), None),
        P(("shard", "context"), "tensor"),
        P(("shard", "context"), "tensor"),
        P(("shard", "context"), None),
        P(("shard", "context"), "tensor"),
        P("tensor", ("shard", "context")),
        P(),
        P(None, "tensor"),
        P("tensor"),
        P(),
        P(),
        P("tensor"),
        P("tensor"),
        P("tensor"),
        P("tensor"),
    )
    return jax.shard_map(shards, mesh=mesh, in_specs=in_specs, out_specs=out_specs, check_vma=False)
```

profile of v0, /device:TPU:0, one launch (start us, length us, event | category | flops | bytes accessed | tf_op | source)
XLA Modules:
  0.0 1078.0 jit_solution(2125863007557966451)
XLA Ops:
  27.7 12.3 %all_gather.36 = bf16[1536,256]{1,0:T(8,128)(2,1)S(1)} all-gather(bf16[384,256]{1,0:T(8,128)(2,1)S(1)} %copy-done.50), channel_id=1, replica_groups=mesh['shard'=4,'context'=2,'tensor'=4] {'shard'}, dimensions={0}, use_global_device_ids=true | all-gather | bytes 983040 | tf_op jit(solution)/shard_map/all_gather | solution.py:142
  116.2 10.8 all-gather.1
  133.1 14.4 %bitcast_add_fusion.4 = f32[4,256,12,64]{1,3,2,0:T(8,128)S(1)} fusion(f32[4,256,12,64]{1,3,2,0:T(8,128)S(1)} %fusion.67, f32[4,256,256]{2,1,0:T(8,128)S(1)} %fusion.129, f32[4,12,256]{2,1,0:T(8,128)S(1)} %copy-done.32, pred[256,256]{1,0:T(8,128)(4,1)S(1)} %copy-done.53, f32[4,256,12,64]{1,0,3,2:T(4,128)S(1)} %copy-done.6, f32[4,256,12]{1,2,0:T(8,128)S(1)} %copy-done.43, ...), kind=kOutput, calls=%fused_computation.75 | convolution fusion | flops 2430861312 | bytes 10698752 | tf_op jit(solution)/shard_map/chts,cshp->cthp/dot_general | solution.py:84
  159.9 11.7 %psum.98 = f32[1024]{0:T(1024)S(1)} all-reduce(f32[1024]{0:T(1024)S(1)} %get-tuple-element.403), channel_id=1, replica_groups=mesh['shard'=4,'context'=2,'tensor'=4] {'tensor'}, use_global_device_ids=true, to_apply=%region_8.9 | all-reduce | flops 1024 | bytes 8192 | tf_op jit(solution)/shard_map/psum | solution.py:180
  171.6 8.6 multiply_reduce_fusion.4
  180.2 8.7 psum.100
  188.9 8.5 multiply_reduce_fusion.5
  219.6 8.7 all-gather.2
  230.2 14.7 %while.60 = (s32[]{:T(128)}, f32[12,64,128]{2,1,0:T(8,128)S(1)}, f32[4,12,64,128]{3,2,1,0:T(8,128)}, f32[4,12]{1,0:T(4,128)}, f32[4,12,1,1]{1,3,2,0:T(1,128)}, /...) while((s32[]{:T(128)}, f32[12,64,128]{2,1,0:T(8,128)S(1)}, ...), condition=%wide.region_13.14_spmd.clone, body=%wide.region_12.13_spmd.clone.sunk | while | flops 393219 | bytes 1967968 | solution.py:66
  248.8 18.7 %while.58 = (s32[]{:T(128)}, f32[12,64,128]{2,1,0:T(8,128)S(1)}, f32[4,12]{1,0:T(4,128)}, f32[4,12,64,128]{3,2,1,0:T(8,128)}, f32[4,12,64,128]{3,2,1,0:T(8,128)}...) while((s32[]{:T(128)}, f32[12,64,128]{2,1,0:T(8,128)S(1)}, ...), condition=%wide.region_16.17_spmd, body=%wide.region_14.16_spmd.sunk | while | flops 393219 | bytes 2359869 | solution.py:66
  278.9 20.5 %fusion.60 = (f32[4,12,256]{2,1,0:T(8,128)S(1)}, f32[4,12,256]{2,1,0:T(8,128)}, f32[4,256,256]{2,1,0:T(8,128)S(1)}) fusion(f32[4,12,256]{2,1,0:T(8,128)S(1)} %copy-done.33, f32[4,256,256]{2,1,0:T(8,128)S(1)} %copy-done.40, pred[256,256]{1,0:T(8,128)(4,1)S(1)} %copy-done.54, f32[4,256,12,64]{1,0,3,2:T(4,128)S(1)} %copy-done.7, ...), kind=kOutput, calls=%fused_computation.106 | convolution fusion | flops 2463604736 | bytes 8650752 | tf_op jit(solution)/shard_map/transpose(jvp(chts,cshp->cthp))/dot_general | solution.py:84
  308.7 12.6 %bitcast_add_fusion.3 = f32[4,256,12,64]{1,3,2,0:T(8,128)} fusion(f32[4,256,12,64]{1,3,2,0:T(8,128)S(1)} %get-tuple-element.434, f32[4,256,256]{2,1,0:T(8,128)S(1)} %copy-done.40, f32[4,12,256]{2,1,0:T(8,128)S(1)} %copy-done.33, pred[256,256]{1,0:T(8,128)(4,1)S(1)} %copy-done.54, f32[4,256,12,64]{1,0,3,2:T(4,128)S(1)} %copy-done.8, ...), kind=kOutput, calls=%fused_computation.71 | convolution fusion | flops 2430074880 | bytes 10649600 | tf_op jit(solution)/shard_map/transpose(jvp(chts,cshp->cthp))/dot_general | solution.py:84
  335.8 9.9 reduce-window.16
  375.2 8.6 all-reduce.14.cloned.1.call-done
  383.8 12.4 %multiply_reduce_fusion.3 = (f32[1024]{0:T(1024)S(1)}, f32[1024]{0:T(1024)S(1)}, f32[1024]{0:T(1024)S(1)}, f32[1024]{0:T(1024)S(1)}, f32[1024]{0:T(1024)S(1)}, /*index=5*/f32[1024,1024]{0,1:T(8,128)S(1)}) fusion(f32[1027,1024]{0,1:T(8,128)} %copy-done, f32[1024,1024]{0,1:T(8,128)} %get-tuple-element.406, f32[1024,256]{0,1:T(8,128)} %all-reduce.14.cloned.1.call-done, ...), kind=kLoop, calls=%fused_computation.65 | loop fusion | flops 18869248 | bytes 29380608 | tf_op jit(solution)/shard_map/reduce_sum | solution.py:222
  402.1 9.5 pad_add_fusion
  423.1 8.1 add_add_fusion
  458.7 397.3 %all-reduce.16.cloned.1.call-done = (f32[1024,1536]{1,0:T(8,128)}, f32[1024,1536]{1,0:T(8,128)}) async-done(((f32[1024,1536]{1,0:T(8,128)}, f32[1024,1536]{1,0:T(8,128)}), (f32[1024,1536]{1,0:T(8,128)}, f32[1024,1536]{1,0:T(8,128)})) %all-reduce.16.cloned.1.call-update) | async-done | bytes 12582928 | tf_op jit(solution)/shard_map/psum | solution.py:184
  856.0 8.2 fusion.27
  864.2 25.9 %all-reduce.9 = (f32[1536]{0:T(1024)}, f32[4,768]{1,0:T(4,128)}, f32[768]{0:T(1024)}, f32[4,256]{1,0:T(4,128)}, f32[256]{0:T(256)}, /*index=5*/f32[12]{0:T(128)}, f32[12]{0:T(128)}, f32[12]{0:T(128)}, f32[768]{0:T(1024)}) all-reduce(f32[1536]{0:T(1024)S(1)} %get-tuple-element.332, ...), channel_id=1, replica_groups=mesh['shard'=4,'context'=2,'tensor'=4] {'shard','context'}, use_global_device_ids=true, to_apply=%region_38.39 | all-reduce | flops 7460 | bytes 59680 | tf_op jit(solution)/shard_map/psum | solution.py:273
  890.1 9.2 fusion.22
  899.3 56.2 %reduce-scatter.14.cloned.1.call-done = f32[768,192]{0,1:T(8,128)} async-done(((f32[768,1536]{0,1:T(8,128)}), f32[768,192]{0,1:T(8,128)}) %reduce-scatter.14.cloned.1.call-update) | async-done | bytes 589840 | tf_op jit(solution)/shard_map/reduce_scatter | solution.py:261
  955.5 57.8 %reduce-scatter.8.cloned.1.call-done = f32[192,768]{1,0:T(8,128)} async-done(((f32[1536,768]{1,0:T(8,128)}), f32[192,768]{1,0:T(8,128)}) %reduce-scatter.8.cloned.1.call-update) | async-done | bytes 589840 | tf_op jit(solution)/shard_map/reduce_scatter | solution.py:257
  1013.3 57.7 %reduce-scatter.10.cloned.1.call-done = f32[192,768]{1,0:T(8,128)} async-done(((f32[1536,768]{1,0:T(8,128)}), f32[192,768]{1,0:T(8,128)}) %reduce-scatter.10.cloned.1.call-update) | async-done | bytes 589840 | tf_op jit(solution)/shard_map/reduce_scatter | solution.py:258
  (397 shorter events, 291.9 us)
Async XLA Ops:
  7.2 45.0 %all-gather.7.cloned.1.call-start = ((), (), s32[]{:S(2)}) async-start(), calls=%async_computation.5 | async-start | bytes 2949120 | tf_op jit(solution)/shard_map/all_gather | solution.py:141
  8.0 144.0 %all-gather.9.cloned.1.call-start = ((), (), s32[]{:S(2)}) async-start(), calls=%async_computation.6 | async-start | bytes 2949120 | tf_op jit(solution)/shard_map/all_gather | solution.py:140
  8.7 162.9 %all-gather.11.cloned.1.call-start = ((), (), s32[]{:S(2)}) async-start(), calls=%async_computation.7 | async-start | bytes 2949120 | tf_op jit(solution)/shard_map/all_gather | solution.py:144
  9.4 374.3 %all-reduce.14.cloned.1.call-start = ((), (), s32[]{:S(2)}) async-start(), calls=%async_computation.8 | async-start | bytes 2097152 | tf_op jit(solution)/shard_map/psum | solution.py:217
  26.5 19.9 %copy-start.85 = (f32[12]{0:T(128)}, f32[12]{0:T(128)S(1)}, u32[]{:S(2)}) copy-start(f32[12]{0:T(128)S(1)} %get-tuple-element.342) | copy-start | bytes 148
  27.6 24.6 %copy-start.4 = (bf16[1024,1536]{1,0:T(8,128)(2,1)S(1)}, bf16[1024,1536]{1,0:T(8,128)(2,1)}, u32[]{:S(2)}) copy-start(bf16[1024,1536]{1,0:T(8,128)(2,1)} %copy-done.3) | copy-start | bytes 9437188
  45.2 28.5 %copy-start.59 = (f32[1,1024]{1,0:T(1,128)}, f32[1,1024]{1,0:T(1,128)S(1)}, u32[]{:S(2)}) copy-start(f32[1,1024]{1,0:T(1,128)S(1)} %get-tuple-element.424) | copy-start | bytes 12292
  57.7 13.2 %collective-permute-start = (bf16[3,1024]{0,1:T(8,128)(2,1)}, bf16[3,1024]{0,1:T(8,128)(2,1)}, u32[]{:S(2)}, u32[]{:S(2)}) collective-permute-start(bf16[3,1024]{0,1:T(8,128)(2,1)} %pad_maximum_fusion.1), channel_id=1, source_target_pairs={{0,4},{1,5},{2,6},{3,7},{8,12},{9,13},{10,14},{11,15},{16,20},{17,... | collective-permute-start | bytes 18440 | tf_op jit(solution)/shard_map/ppermute | solution.py:18
  67.2 121.8 %copy-start.57 = (f32[768]{0:T(1024)}, f32[768]{0:T(1024)S(1)}, u32[]{:S(2)}) copy-start(f32[768]{0:T(1024)S(1)} %mul.593) | copy-start | bytes 9220
  128.0 72.4 %copy-start.16 = (f32[12,64,128]{2,1,0:T(8,128)}, f32[12,64,128]{2,1,0:T(8,128)S(1)}, u32[]{:S(2)}) copy-start(f32[12,64,128]{2,1,0:T(8,128)S(1)} %fusion.102) | copy-start | bytes 1179652
  278.9 20.5 %copy-start.13 = (f32[4,12,64,128]{3,2,1,0:T(8,128)S(1)}, f32[4,12,64,128]{3,2,1,0:T(8,128)}, u32[]{:S(2)}) copy-start(f32[4,12,64,128]{3,2,1,0:T(8,128)} %get-tuple-element.666) | copy-start | bytes 4718596
  278.9 20.5 %copy-start.17 = (f32[12,64,128]{2,1,0:T(8,128)S(1)}, f32[12,64,128]{2,1,0:T(8,128)}, u32[]{:S(2)}) copy-start(f32[12,64,128]{2,1,0:T(8,128)} %copy-done.16) | copy-start | bytes 1179652
  278.9 20.5 %copy-start.44 = (f32[4,256,12]{1,2,0:T(8,128)S(1)}, f32[4,256,12]{1,2,0:T(8,128)}, u32[]{:S(2)}) copy-start(f32[4,256,12]{1,2,0:T(8,128)} %get-tuple-element.421) | copy-start | bytes 147460
  299.4 22.0 %copy-start.27 = (f32[4,256,256]{2,1,0:T(8,128)}, f32[4,256,256]{2,1,0:T(8,128)S(1)}, u32[]{:S(2)}) copy-start(f32[4,256,256]{2,1,0:T(8,128)S(1)} %get-tuple-element.331) | copy-start | bytes 3145732
  333.9 123.0 %reduce-scatter.16.cloned.1.call-start = ((), (), s32[]{:S(2)}) async-start(), calls=%async_computation.13 | async-start | bytes 884736
  363.6 492.4 %all-reduce.16.cloned.1.call-start = ((), (), s32[]{:S(2)}) async-start(), calls=%async_computation.14 | async-start | bytes 25165824 | tf_op jit(solution)/shard_map/psum | solution.py:184
  400.8 17.8 %collective-permute-start.1 = (f32[3,1024]{0,1:T(8,128)S(1)}, f32[3,1024]{0,1:T(8,128)S(1)}, u32[]{:S(2)}, u32[]{:S(2)}) collective-permute-start(f32[3,1024]{0,1:T(8,128)S(1)} %pad_add_fusion.1), channel_id=1, source_target_pairs={{4,0},{5,1},{6,2},{7,3},{12,8},{13,9},{14,10},{15,11},{20,16},{21,... | collective-permute-start | bytes 36872 | tf_op jit(solution)/shard_map/ppermute | solution.py:18
  431.2 468.1 %reduce-scatter.12.cloned.1.call-start = ((), (), s32[]{:S(2)}) async-start(), calls=%async_computation.11 | async-start | bytes 1769472 | tf_op jit(solution)/shard_map/reduce_scatter | solution.py:259
  436.3 519.1 %reduce-scatter.14.cloned.1.call-start = ((), (), s32[]{:S(2)}) async-start(), calls=%async_computation.12 | async-start | bytes 5308416 | tf_op jit(solution)/shard_map/reduce_scatter | solution.py:261
  444.4 568.9 %reduce-scatter.8.cloned.1.call-start = ((), (), s32[]{:S(2)}) async-start(), calls=%async_computation.9 | async-start | bytes 5308416 | tf_op jit(solution)/shard_map/reduce_scatter | solution.py:257
  450.2 620.8 %reduce-scatter.10.cloned.1.call-start = ((), (), s32[]{:S(2)}) async-start(), calls=%async_computation.10 | async-start | bytes 5308416 | tf_op jit(solution)/shard_map/reduce_scatter | solution.py:258
  456.0 400.0 %copy-start.2 = (bf16[1024,1536]{1,0:T(8,128)(2,1)S(1)}, bf16[1024,1536]{1,0:T(8,128)(2,1)}, u32[]{:S(2)}) copy-start(bf16[1024,1536]{1,0:T(8,128)(2,1)} %param.22) | copy-start | bytes 9437188
  456.0 400.0 %copy-start.52 = (f32[1536]{0:T(1024)S(1)}, f32[1536]{0:T(1024)}, u32[]{:S(2)}) copy-start(f32[1536]{0:T(1024)} %param.23) | copy-start | bytes 18436
  456.0 400.0 %copy-start.56 = (f32[1024]{0:T(1024)S(1)}, f32[1024]{0:T(1024)}, u32[]{:S(2)}) copy-start(f32[1024]{0:T(1024)} %copy-done.55) | copy-start | bytes 12292
  (81 other events, 549.0 us)
Sparse Core Ops, SparseCore 0:
  9.6 29.9 all-gather.6
  41.1 23.6 all-gather.8
  66.4 24.0 all-gather.10
  334.0 49.6 all-reduce.13
  386.7 36.3 reduce-scatter.15
  431.3 424.6 all-reduce.15
  859.9 37.7 reduce-scatter.11
  901.7 53.7 reduce-scatter.13
  959.5 53.7 reduce-scatter.7
  1017.2 53.7 reduce-scatter.9
where the time goes:
time: 1090 us; the launch traced here: 1080 us
  waiting for transfers between devices  587 us (54%)
  matrix products  181 us (17%)
  other arithmetic  106 us (10%)
  local copies, waits for them, and re-layouts  91.8 us (8%)
  blocking collectives  89.3 us (8%)
  between operations  16.3 us (1%)
    psum x1, waiting for transfers between devices, shards(): out_total = lax.psum(out_part, 'tensor')  397 us
    reduce_scatter x1, waiting for transfers between devices, shards(): lax.psum_scatter(grad_w_z, ('shard', 'context'), scatter_dimension=0, til...  57.8 us
    reduce_scatter x1, waiting for transfers between devices, shards(): lax.psum_scatter(grad_w_x, ('shard', 'context'), scatter_dimension=0, til...  57.7 us
    reduce_scatter x1, waiting for transfers between devices, shards(): lax.psum_scatter(grad_w_out, ('shard', 'context'), scatter_dimension=1, t...  56.2 us
    dot_general x3, matrix products, group_output(): jnp.einsum('chts,cshp->cthp', decay * scores[:, None], x_step, precision=...  47.5 us
    psum x1, blocking collectives, shards(): lax.psum((grad_norm_gain, grad_conv_weight[:, :local_inner], grad_conv_bi...  25.9 us
  transfers between devices with their start and end apart: 12, of which 6 were waited for; matrix products, arithmetic and copies ran while one was open for 21% of the time, Pallas kernels for 0%

commit v1 on v0

--- a/solution.py
+++ b/solution.py
@@ -181,7 +181,7 @@
     gate_inverse = lax.rsqrt(square_sum[:, None] / inner_width + epsilon)
     gated_out = (gated * gate_inverse * gate_gain).astype(jnp.bfloat16)
     out_part = jnp.dot(gated_out, full_out, preferred_element_type=jnp.float32)
-    out_total = lax.psum(out_part, "tensor")
+    out_total = jnp.sum(lax.all_gather(out_part, "tensor"), axis=0)
     block_output = (x_float + out_total).astype(jnp.bfloat16)
     grad_gated_out = jnp.einsum(
         "td,kd->tk", out_cotangent, full_out, preferred_element_type=jnp.float32

time: 1090 us -> 1310 us (1.20)
  waiting for transfers between devices: 587 us -> 789 us
  other arithmetic: 106 us -> 120 us
    all_gather x0 -> x1, waiting for transfers between devices: none -> 391 us  [shards(): out_total = jnp.sum(lax.all_gather(out_part, 'tensor'), axis=0)]
    psum x1, waiting for transfers between devices: 397 us -> 186 us  [shards(): lax.psum(partial_normed, 'tensor')]
    reduce_scatter x1, waiting for transfers between devices: 0.01 us -> 18 us  [shards(): lax.psum_scatter(grad_w_bc, ('shard', 'context'), scatter_dimension=0, ti...]
    reduce_sum x0 -> x1, other arithmetic: none -> 13.3 us  [shards(): out_total = jnp.sum(lax.all_gather(out_part, 'tensor'), axis=0)]
  transfers between devices with their start and end apart: 12 -> 13, of which waited for: 6 -> 8; matrix products, arithmetic and copies ran while one was open for 21% -> 18% of each run, Pallas kernels for 0% -> 0%
where the time goes in v1:
time: 1310 us; the launch traced here: 1300 us
  waiting for transfers between devices  789 us (60%)
  matrix products  184 us (14%)
  other arithmetic  120 us (9%)
  local copies, waits for them, and re-layouts  93.5 us (7%)
  blocking collectives  88.9 us (7%)
  between operations  16 us (1%)
    all_gather x1, waiting for transfers between devices, shards(): out_total = jnp.sum(lax.all_gather(out_part, 'tensor'), axis=0)  391 us
    psum x1, waiting for transfers between devices, shards(): lax.psum(partial_normed, 'tensor')  186 us
    reduce_scatter x1, waiting for transfers between devices, shards(): lax.psum_scatter(grad_w_out, ('shard', 'context'), scatter_dimension=1, t...  57.8 us
    reduce_scatter x1, waiting for transfers between devices, shards(): lax.psum_scatter(grad_w_x, ('shard', 'context'), scatter_dimension=0, til...  57.8 us
    reduce_scatter x1, waiting for transfers between devices, shards(): lax.psum_scatter(grad_w_z, ('shard', 'context'), scatter_dimension=0, til...  57.7 us
    dot_general x3, matrix products, group_output(): jnp.einsum('chts,cshp->cthp', decay * scores[:, None], x_step, precision=...  47.4 us
  transfers between devices with their start and end apart: 13, of which 8 were waited for; matrix products, arithmetic and copies ran while one was open for 18% of the time, Pallas kernels for 0%

profile of v1, /device:TPU:0, one launch (start us, length us, event | category | flops | bytes accessed | tf_op | source)
XLA Modules:
  0.0 1298.9 jit_solution(2627003078814106697)
XLA Ops:
  27.6 12.3 all_gather.42
  115.7 10.9 all-gather.1
  132.8 14.6 %bitcast_add_fusion.4 = f32[4,256,12,64]{1,3,2,0:T(8,128)S(1)} fusion(f32[4,256,12,64]{1,3,2,0:T(8,128)S(1)} %fusion.67, f32[4,256,256]{2,1,0:T(8,128)S(1)} %fusion.129, f32[4,12,256]{2,1,0:T(8,128)S(1)} %copy-done.32, pred[256,256]{1,0:T(8,128)(4,1)S(1)} %copy-done.52, f32[4,256,12,64]{1,0,3,2:T(4,128)S(1)} %copy-done.6, f32[4,256,12]{1,2,0:T(8,128)S(1)} %copy-done.42, ...), kind=kOutput, calls=%fused_computation.75 | convolution fusion | flops 2430861312 | bytes 10698752 | tf_op jit(solution)/shard_map/chts,cshp->cthp/dot_general | solution.py:84
  159.7 11.7 psum.91
  171.4 8.7 multiply_reduce_fusion.4
  219.2 8.8 all-gather.3
  229.9 14.8 %while.60 = (s32[]{:T(128)}, f32[12,64,128]{2,1,0:T(8,128)S(1)}, f32[4,12,64,128]{3,2,1,0:T(8,128)}, f32[4,12]{1,0:T(4,128)}, f32[4,12,1,1]{1,3,2,0:T(1,128)}, /...) while((s32[]{:T(128)}, f32[12,64,128]{2,1,0:T(8,128)S(1)}, ...), condition=%wide.region_13.14_spmd.clone, body=%wide.region_12.13_spmd.clone.sunk | while | flops 393219 | bytes 1967968 | solution.py:66
  248.6 18.8 %while.58 = (s32[]{:T(128)}, f32[12,64,128]{2,1,0:T(8,128)S(1)}, f32[4,12]{1,0:T(4,128)}, f32[4,12,64,128]{3,2,1,0:T(8,128)}, f32[4,12,64,128]{3,2,1,0:T(8,128)}...) while((s32[]{:T(128)}, f32[12,64,128]{2,1,0:T(8,128)S(1)}, ...), condition=%wide.region_16.17_spmd, body=%wide.region_14.16_spmd.sunk | while | flops 393219 | bytes 2359869 | solution.py:66
  278.7 20.5 %fusion.60 = (f32[4,12,256]{2,1,0:T(8,128)S(1)}, f32[4,12,256]{2,1,0:T(8,128)}, f32[4,256,256]{2,1,0:T(8,128)S(1)}) fusion(f32[4,12,256]{2,1,0:T(8,128)S(1)} %copy-done.33, f32[4,256,256]{2,1,0:T(8,128)S(1)} %copy-done.39, pred[256,256]{1,0:T(8,128)(4,1)S(1)} %copy-done.53, f32[4,256,12,64]{1,0,3,2:T(4,128)S(1)} %copy-done.7, ...), kind=kOutput, calls=%fused_computation.106 | convolution fusion | flops 2463604736 | bytes 8650752 | tf_op jit(solution)/shard_map/transpose(jvp(chts,cshp->cthp))/dot_general | solution.py:84
  308.6 12.4 bitcast_add_fusion.3
  335.4 9.9 reduce-window.16
  371.4 11.9 all-reduce.13.cloned.1.call-done
  383.3 13.0 %multiply_reduce_fusion.3 = (f32[1024]{0:T(1024)S(1)}, f32[1024]{0:T(1024)S(1)}, f32[1024]{0:T(1024)S(1)}, f32[1024]{0:T(1024)S(1)}, f32[1024]{0:T(1024)S(1)}, /*index=5*/f32[1024,1024]{0,1:T(8,128)S(1)}) fusion(f32[1027,1024]{0,1:T(8,128)} %copy-done, f32[1024,1024]{0,1:T(8,128)} %get-tuple-element.404, f32[1024,256]{0,1:T(8,128)} %all-reduce.13.cloned.1.call-done, ...), kind=kLoop, calls=%fused_computation.65 | loop fusion | flops 18869248 | bytes 29380608 | tf_op jit(solution)/shard_map/reduce_sum | solution.py:222
  402.3 9.7 pad_add_fusion
  467.1 185.6 %all-reduce.15.cloned.1.call-done = f32[1024,1536]{1,0:T(8,128)} async-done(((f32[1024,1536]{1,0:T(8,128)}), f32[1024,1536]{1,0:T(8,128)}) %all-reduce.15.cloned.1.call-update) | async-done | bytes 6291472 | tf_op jit(solution)/shard_map/psum | solution.py:238
  652.7 8.7 fusion.27
  661.4 25.5 %all-reduce.9 = (f32[1536]{0:T(1024)}, f32[4,768]{1,0:T(4,128)}, f32[768]{0:T(1024)}, f32[4,256]{1,0:T(4,128)}, f32[256]{0:T(256)}, /*index=5*/f32[12]{0:T(128)}, f32[12]{0:T(128)}, f32[12]{0:T(128)}, f32[768]{0:T(1024)}) all-reduce(f32[1536]{0:T(1024)S(1)} %get-tuple-element.332, ...), channel_id=1, replica_groups=mesh['shard'=4,'context'=2,'tensor'=4] {'shard','context'}, use_global_device_ids=true, to_apply=%region_38.39 | all-reduce | flops 7460 | bytes 59680 | tf_op jit(solution)/shard_map/psum | solution.py:273
  686.9 391.5 %all-gather.15.cloned.1.call-done = f32[4096,1536]{1,0:T(8,128)} async-done(((f32[1024,1536]{1,0:T(8,128)}), f32[4096,1536]{1,0:T(8,128)}) %all-gather.15.cloned.1.call-update) | async-done | bytes 25165840 | tf_op jit(solution)/shard_map/all_gather | solution.py:184
  1078.4 13.3 %reduce_sum.290 = f32[1024,1536]{1,0:T(8,128)} reduce(f32[4,1024,1536]{2,1,0:T(8,128)} %bitcast.216, f32[]{:T(128)} %constant.135.clone.1), dimensions={0}, to_apply=%region_9.10 | reduce | flops 4718592 | bytes 31457284 | tf_op jit(solution)/shard_map/reduce_sum | solution.py:184
  1091.7 9.1 fusion.22
  1100.8 18.0 %reduce-scatter.12.cloned.1.call-done = f32[192,256]{1,0:T(8,128)} async-done(((f32[1536,256]{1,0:T(8,128)}), f32[192,256]{1,0:T(8,128)}) %reduce-scatter.12.cloned.1.call-update) | async-done | bytes 196624 | tf_op jit(solution)/shard_map/reduce_scatter | solution.py:259
  1118.8 57.8 %reduce-scatter.14.cloned.1.call-done = f32[768,192]{0,1:T(8,128)} async-done(((f32[768,1536]{0,1:T(8,128)}), f32[768,192]{0,1:T(8,128)}) %reduce-scatter.14.cloned.1.call-update) | async-done | bytes 589840 | tf_op jit(solution)/shard_map/reduce_scatter | solution.py:261
  1176.6 57.7 %reduce-scatter.8.cloned.1.call-done = f32[192,768]{1,0:T(8,128)} async-done(((f32[1536,768]{1,0:T(8,128)}), f32[192,768]{1,0:T(8,128)}) %reduce-scatter.8.cloned.1.call-update) | async-done | bytes 589840 | tf_op jit(solution)/shard_map/reduce_scatter | solution.py:257
  1234.3 57.8 %reduce-scatter.10.cloned.1.call-done = f32[192,768]{1,0:T(8,128)} async-done(((f32[1536,768]{1,0:T(8,128)}), f32[192,768]{1,0:T(8,128)}) %reduce-scatter.10.cloned.1.call-update) | async-done | bytes 589840 | tf_op jit(solution)/shard_map/reduce_scatter | solution.py:258
  (397 shorter events, 321.1 us)
Async XLA Ops:
  7.2 45.0 %all-gather.9.cloned.1.call-start = ((), (), s32[]{:S(2)}) async-start(), calls=%async_computation.5 | async-start | bytes 2949120 | tf_op jit(solution)/shard_map/all_gather | solution.py:141
  8.0 143.8 %all-gather.11.cloned.1.call-start = ((), (), s32[]{:S(2)}) async-start(), calls=%async_computation.6 | async-start | bytes 2949120 | tf_op jit(solution)/shard_map/all_gather | solution.py:140
  8.7 162.7 %all-gather.13.cloned.1.call-start = ((), (), s32[]{:S(2)}) async-start(), calls=%async_computation.7 | async-start | bytes 2949120 | tf_op jit(solution)/shard_map/all_gather | solution.py:144
  9.4 373.9 %all-reduce.13.cloned.1.call-start = ((), (), s32[]{:S(2)}) async-start(), calls=%async_computation.8 | async-start | bytes 2097152 | tf_op jit(solution)/shard_map/psum | solution.py:217
  27.6 24.6 %copy-start.4 = (bf16[1024,1536]{1,0:T(8,128)(2,1)S(1)}, bf16[1024,1536]{1,0:T(8,128)(2,1)}, u32[]{:S(2)}) copy-start(bf16[1024,1536]{1,0:T(8,128)(2,1)} %copy-done.3) | copy-start | bytes 9437188
  45.2 28.2 %copy-start.58 = (f32[1,1024]{1,0:T(1,128)}, f32[1,1024]{1,0:T(1,128)S(1)}, u32[]{:S(2)}) copy-start(f32[1,1024]{1,0:T(1,128)S(1)} %get-tuple-element.422) | copy-start | bytes 12292
  57.7 12.9 collective-permute-start
  66.9 121.7 %copy-start.56 = (f32[768]{0:T(1024)}, f32[768]{0:T(1024)S(1)}, u32[]{:S(2)}) copy-start(f32[768]{0:T(1024)S(1)} %mul.593) | copy-start | bytes 9220
  127.6 72.4 %copy-start.16 = (f32[12,64,128]{2,1,0:T(8,128)}, f32[12,64,128]{2,1,0:T(8,128)S(1)}, u32[]{:S(2)}) copy-start(f32[12,64,128]{2,1,0:T(8,128)S(1)} %fusion.102) | copy-start | bytes 1179652
  278.7 20.5 %copy-start.13 = (f32[4,12,64,128]{3,2,1,0:T(8,128)S(1)}, f32[4,12,64,128]{3,2,1,0:T(8,128)}, u32[]{:S(2)}) copy-start(f32[4,12,64,128]{3,2,1,0:T(8,128)} %get-tuple-element.662) | copy-start | bytes 4718596
  278.7 20.5 %copy-start.17 = (f32[12,64,128]{2,1,0:T(8,128)S(1)}, f32[12,64,128]{2,1,0:T(8,128)}, u32[]{:S(2)}) copy-start(f32[12,64,128]{2,1,0:T(8,128)} %copy-done.16) | copy-start | bytes 1179652
  299.2 21.8 %copy-start.27 = (f32[4,256,256]{2,1,0:T(8,128)}, f32[4,256,256]{2,1,0:T(8,128)S(1)}, u32[]{:S(2)}) copy-start(f32[4,256,256]{2,1,0:T(8,128)S(1)} %get-tuple-element.331) | copy-start | bytes 3145732
  333.5 131.8 %reduce-scatter.16.cloned.1.call-start = ((), (), s32[]{:S(2)}) async-start(), calls=%async_computation.15 | async-start | bytes 884736
  363.3 289.4 %all-reduce.15.cloned.1.call-start = ((), (), s32[]{:S(2)}) async-start(), calls=%async_computation.9 | async-start | bytes 12582912 | tf_op jit(solution)/shard_map/psum | solution.py:238
  401.0 17.8 %collective-permute-start.1 = (f32[3,1024]{0,1:T(8,128)S(1)}, f32[3,1024]{0,1:T(8,128)S(1)}, u32[]{:S(2)}, u32[]{:S(2)}) collective-permute-start(f32[3,1024]{0,1:T(8,128)S(1)} %pad_add_fusion.1), channel_id=1, source_target_pairs={{4,0},{5,1},{6,2},{7,3},{12,8},{13,9},{14,10},{15,11},{20,16},{21,... | collective-permute-start | bytes 36872 | tf_op jit(solution)/shard_map/ppermute | solution.py:18
  431.2 647.2 %all-gather.15.cloned.1.call-start = ((), (), s32[]{:S(2)}) async-start(), calls=%async_computation.14 | async-start | bytes 31457280 | tf_op jit(solution)/shard_map/all_gather | solution.py:184
  439.5 679.3 %reduce-scatter.12.cloned.1.call-start = ((), (), s32[]{:S(2)}) async-start(), calls=%async_computation.12 | async-start | bytes 1769472 | tf_op jit(solution)/shard_map/reduce_scatter | solution.py:259
  444.6 732.0 %reduce-scatter.14.cloned.1.call-start = ((), (), s32[]{:S(2)}) async-start(), calls=%async_computation.13 | async-start | bytes 5308416 | tf_op jit(solution)/shard_map/reduce_scatter | solution.py:261
  452.5 781.8 %reduce-scatter.8.cloned.1.call-start = ((), (), s32[]{:S(2)}) async-start(), calls=%async_computation.10 | async-start | bytes 5308416 | tf_op jit(solution)/shard_map/reduce_scatter | solution.py:257
  458.6 833.5 %reduce-scatter.10.cloned.1.call-start = ((), (), s32[]{:S(2)}) async-start(), calls=%async_computation.11 | async-start | bytes 5308416 | tf_op jit(solution)/shard_map/reduce_scatter | solution.py:258
  464.3 188.4 %copy-start.2 = (bf16[1024,1536]{1,0:T(8,128)(2,1)S(1)}, bf16[1024,1536]{1,0:T(8,128)(2,1)}, u32[]{:S(2)}) copy-start(bf16[1024,1536]{1,0:T(8,128)(2,1)} %param.22) | copy-start | bytes 9437188
  464.3 188.4 %copy-start.51 = (f32[1536]{0:T(1024)S(1)}, f32[1536]{0:T(1024)}, u32[]{:S(2)}) copy-start(f32[1536]{0:T(1024)} %param.23) | copy-start | bytes 18436
  464.4 188.4 %copy-start.55 = (f32[1024]{0:T(1024)S(1)}, f32[1024]{0:T(1024)}, u32[]{:S(2)}) copy-start(f32[1024]{0:T(1024)} %copy-done.54) | copy-start | bytes 12292
  467.1 194.3 %copy-start.79 = (f32[768]{0:T(1024)S(1)}, f32[768]{0:T(1024)}, u32[]{:S(2)}) copy-start(f32[768]{0:T(1024)} %get-tuple-element.338) | copy-start | bytes 9220
  (80 other events, 569.7 us)
Sparse Core Ops, SparseCore 0:
  9.6 29.9 all-gather.8
  41.1 23.6 all-gather.10
  66.4 24.0 all-gather.12
  333.6 49.6 all-reduce.12
  386.3 36.3 reduce-scatter.15
  431.3 221.3 all-reduce.14
  654.3 424.0 all-gather.14
  1082.2 36.5 reduce-scatter.11
  1122.8 53.7 reduce-scatter.13
  1180.5 53.7 reduce-scatter.7
  1238.3 53.7 reduce-scatter.9
